TPU v7x, 32 devices: a whole 2x2x4 slice. The times are simulated.
32 devices in a mesh: seq: 8 (over z, x), head: 4 (over y, core).
Axes of the slice: x: 2, y: 2, z: 4, core: 2. Of those that a mesh axis runs over, the one named last changes fastest.
Arguments:
- queries: bfloat16 [2048, 512], P('seq', 'head'), may hold values from -16 to 16
- keys: bfloat16 [2048, 512], P(('seq', 'head')), may hold values from -16 to 16
- values: bfloat16 [2048, 512], P(('seq', 'head')), may hold values from -6 to 6
- out_grad: bfloat16 [2048, 512], P('seq', 'head'), may hold values from -6 to 6
Outputs:
- attended: bfloat16 [2048, 512], P('seq', 'head')
- query_grad: float32 [2048, 512], P('seq', 'head')
- key_grad: float32 [2048, 512], P('seq', 'head')
- value_grad: float32 [2048, 512], P('seq', 'head')
All inputs are finite; a program needn't handle non-finite values.
Results may differ from a plain program's by a relative error of at most 0.0095.
Values may be sent and summed in bfloat16 or wider, within the bound.
A program may use at most 64 MiB of HBM per device.

v0:
```python
import math

import jax
import jax.numpy as jnp
from jax import lax
from jax.sharding import PartitionSpec as P

masked_value = -1e30


def key_block(length, row_count):
    return min(length, max(1024, 2 * row_count))


def attend_range(queries, qstart, whole_keys, whole_values, key_low, key_high, scaling):
    row_count, head_width = queries.shape
    length = whole_keys.shape[0]
    span_rows = key_block(length, row_count)
    query_pos = qstart + jnp.arange(row_count, dtype=jnp.int32)

    def attend_compute(running, kstart):
        weighted, rowmax, rowsum = running
        key_piece = lax.dynamic_slice_in_dim(whole_keys, kstart, span_rows, 0)
        value_piece = lax.dynamic_slice_in_dim(whole_values, kstart, span_rows, 0)
        key_pos = kstart + jnp.arange(span_rows, dtype=jnp.int32)
        allowed = (
            (key_pos[None, :] <= query_pos[:, None])
            & (key_pos[None, :] >= key_low)
            & (key_pos[None, :] < key_high)
        )
        scores = (
            jnp.einsum("qd,kd->qk", queries, key_piece, preferred_element_type=jnp.float32)
            * scaling
        )
        scores = jnp.where(allowed, scores, masked_value)
        new_max = jnp.maximum(rowmax, jnp.max(scores, axis=1))
        weights = jnp.where(allowed, jnp.exp(scores - new_max[:, None]), 0.0)
        factor = jnp.exp(rowmax - new_max)
        rowsum = rowsum * factor + jnp.sum(weights, axis=1)
        weighted = weighted * factor[:, None] + jnp.dot(
            weights.astype(jnp.bfloat16), value_piece, preferred_element_type=jnp.float32
        )
        return (weighted, new_max, rowsum)

    def attend_advance(counter, running):
        kstart = counter * span_rows
        needed = (
            (kstart < key_high) & (kstart + span_rows > key_low) & (kstart < qstart + row_count)
        )
        return lax.cond(
            needed,
            lambda previous: attend_compute(previous, kstart),
            lambda previous: previous,
            running,
        )

    initial = (
        jnp.zeros((row_count, head_width), jnp.float32),
        jnp.full((row_count,), masked_value, jnp.float32),
        jnp.zeros((row_count,), jnp.float32),
    )
    return lax.fori_loop(0, length // span_rows, attend_advance, initial)


def backward_range(
    queries,
    out_grad,
    log_norm,
    row_delta,
    qstart,
    whole_keys,
    whole_values,
    key_low,
    key_high,
    scaling,
):
    row_count, head_width = queries.shape
    length = whole_keys.shape[0]
    span_rows = key_block(length, row_count)
    query_pos = qstart + jnp.arange(row_count, dtype=jnp.int32)

    def backward_compute(running, kstart):
        query_part, terms = running
        key_piece = lax.dynamic_slice_in_dim(whole_keys, kstart, span_rows, 0)
        value_piece = lax.dynamic_slice_in_dim(whole_values, kstart, span_rows, 0)
        key_pos = kstart + jnp.arange(span_rows, dtype=jnp.int32)
        allowed = (
            (key_pos[None, :] <= query_pos[:, None])
            & (key_pos[None, :] >= key_low)
            & (key_pos[None, :] < key_high)
        )
        scores = (
            jnp.einsum("qd,kd->qk", queries, key_piece, preferred_element_type=jnp.float32)
            * scaling
        )
        probs = jnp.where(allowed, jnp.exp(scores - log_norm[:, None]), 0.0)
        grad_probs = jnp.einsum(
            "qd,kd->qk", out_grad, value_piece, preferred_element_type=jnp.float32
        )
        grad_scores = (probs * (grad_probs - row_delta[:, None]) * scaling).astype(jnp.bfloat16)
        query_part = query_part + jnp.dot(
            grad_scores, key_piece, preferred_element_type=jnp.float32
        )
        return (query_part, terms)

    def backward_advance(counter, running):
        kstart = counter * span_rows
        needed = (
            (kstart < key_high) & (kstart + span_rows > key_low) & (kstart < qstart + row_count)
        )
        return lax.cond(
            needed,
            lambda previous: backward_compute(previous, kstart),
            lambda previous: previous,
            running,
        )

    initial = (jnp.zeros((row_count, head_width), jnp.float32), None)
    return lax.fori_loop(0, length // span_rows, backward_advance, initial)


def key_range(all_rows, all_grads, all_norms, all_deltas, own_keys, own_values, kstart, scaling):
    length = all_rows.shape[0]
    row_count, head_width = own_keys.shape
    span_rows = key_block(length, row_count)
    key_pos = kstart + jnp.arange(row_count, dtype=jnp.int32)

    def key_compute(running, qstart):
        key_total, value_total = running
        query_piece = lax.dynamic_slice_in_dim(all_rows, qstart, span_rows, 0)
        grad_piece = lax.dynamic_slice_in_dim(all_grads, qstart, span_rows, 0)
        norm_piece = lax.dynamic_slice_in_dim(all_norms, qstart, span_rows, 0)
        delta_piece = lax.dynamic_slice_in_dim(all_deltas, qstart, span_rows, 0)
        query_pos = qstart + jnp.arange(span_rows, dtype=jnp.int32)
        allowed = key_pos[None, :] <= query_pos[:, None]
        scores = (
            jnp.einsum("qd,kd->qk", query_piece, own_keys, preferred_element_type=jnp.float32)
            * scaling
        )
        probs = jnp.where(allowed, jnp.exp(scores - norm_piece[:, None]), 0.0)
        grad_probs = jnp.einsum(
            "qd,kd->qk", grad_piece, own_values, preferred_element_type=jnp.float32
        )
        grad_scores = (probs * (grad_probs - delta_piece[:, None]) * scaling).astype(jnp.bfloat16)
        key_total = key_total + jnp.einsum(
            "qk,qd->kd", grad_scores, query_piece, preferred_element_type=jnp.float32
        )
        value_total = value_total + jnp.einsum(
            "qk,qd->kd", probs.astype(jnp.bfloat16), grad_piece, preferred_element_type=jnp.float32
        )
        return (key_total, value_total)

    def key_advance(counter, running):
        qstart = counter * span_rows
        needed = qstart + span_rows > kstart
        return lax.cond(
            needed,
            lambda previous: key_compute(previous, qstart),
            lambda previous: previous,
            running,
        )

    initial = (
        jnp.zeros((row_count, head_width), jnp.float32),
        jnp.zeros((row_count, head_width), jnp.float32),
    )
    return lax.fori_loop(0, length // span_rows, key_advance, initial)


def per_device(queries, keys, values, out_grad):
    row_count, head_width = queries.shape
    scaling = 1.0 / math.sqrt(head_width)
    local_keys, local_values = (
        lax.all_to_all(keys, "head", split_axis=1, concat_axis=0, tiled=True),
        lax.all_to_all(values, "head", split_axis=1, concat_axis=0, tiled=True),
    )
    whole_keys, whole_values = (
        lax.all_gather(local_keys, "seq", axis=0, tiled=True),
        lax.all_gather(local_values, "seq", axis=0, tiled=True),
    )
    length = whole_keys.shape[0]
    device = lax.axis_index("seq")
    qstart = device * row_count
    weighted, rowmax, rowsum = attend_range(
        queries, qstart, whole_keys, whole_values, 0, length, scaling
    )
    output = weighted / rowsum[:, None]
    log_norm = rowmax + jnp.log(rowsum)
    attended = output.astype(jnp.bfloat16)
    row_delta = jnp.sum(out_grad.astype(jnp.float32) * output, axis=1)
    query_grad, unused = backward_range(
        queries, out_grad, log_norm, row_delta, qstart, whole_keys, whole_values, 0, length, scaling
    )
    all_rows, all_grads = (
        lax.all_gather(queries, "seq", axis=0, tiled=True),
        lax.all_gather(out_grad, "seq", axis=0, tiled=True),
    )
    all_norms, all_deltas = (
        lax.all_gather(log_norm, "seq", axis=0, tiled=True),
        lax.all_gather(row_delta, "seq", axis=0, tiled=True),
    )
    key_grad, value_grad = key_range(
        all_rows, all_grads, all_norms, all_deltas, local_keys, local_values, qstart, scaling
    )
    return (attended, query_grad, key_grad, value_grad)


def solution(mesh):
    in_specs = (
        P("seq", "head"),
        P(("seq", "head"), None),
        P(("seq", "head"), None),
        P("seq", "head"),
    )
    out_specs = (P("seq", "head"), P("seq", "head"), P("seq", "head"), P("seq", "head"))
    return jax.shard_map(
        per_device, mesh=mesh, in_specs=in_specs, out_specs=out_specs, check_vma=False
    )
```

profile of v0, /device:TPU:0, one launch (start us, length us, event | category | flops | bytes accessed | tf_op | source)
XLA Modules:
  0.0 191.5 jit_solution(5664182822753147087)
XLA Ops:
  0.6 0.8 copy-done
  2.1 4.3 %all-to-all-start = ((bf16[64,4,128]{2,0,1:T(8,128)(2,1)}), bf16[64,4,128]{2,0,1:T(8,128)(2,1)S(1)}, u32[]{:S(2)}, u32[]{:S(2)}) async-start(bf16[64,4,128]{2,0,1:T(8,128)(2,1)} %copy_bitcast_fusion.1), calls=%async_computation | async-start | bytes 131072 | tf_op jit(solution)/shard_map/all_to_all | solution.py:174
  6.4 32.7 %all_gather.20 = bf16[2048,128]{1,0:T(8,128)(2,1)S(1)} all-gather(bf16[256,128]{1,0:T(8,128)(2,1)} %param.16), channel_id=1, replica_groups=mesh['seq'=8,'head'=4] {'seq'}, dimensions={0}, use_global_device_ids=true | all-gather | bytes 589824 | tf_op jit(solution)/shard_map/all_gather | solution.py:195
  39.1 31.3 %all_gather.22 = bf16[2048,128]{1,0:T(8,128)(2,1)S(1)} all-gather(bf16[256,128]{1,0:T(8,128)(2,1)S(1)} %copy-done.4), channel_id=1, replica_groups=mesh['seq'=8,'head'=4] {'seq'}, dimensions={0}, use_global_device_ids=true | all-gather | bytes 589824 | tf_op jit(solution)/shard_map/all_gather | solution.py:196
  71.1 3.3 %all-to-all-start.1 = ((bf16[64,4,128]{2,0,1:T(8,128)(2,1)}), bf16[64,4,128]{2,0,1:T(8,128)(2,1)S(1)}, u32[]{:S(2)}, u32[]{:S(2)}) async-start(bf16[64,4,128]{2,0,1:T(8,128)(2,1)} %copy_bitcast_fusion), calls=%async_computation.1 | async-start | bytes 131072 | tf_op jit(solution)/shard_map/all_to_all | solution.py:175
  74.4 31.2 %all_gather.18 = bf16[2048,128]{1,0:T(8,128)(2,1)S(1)} all-gather(bf16[256,128]{1,0:T(8,128)(2,1)S(1)} %bitcast.47), channel_id=1, replica_groups=mesh['seq'=8,'head'=4] {'seq'}, dimensions={0}, use_global_device_ids=true | all-gather | bytes 589824 | tf_op jit(solution)/shard_map/all_gather | solution.py:178
  105.6 31.5 %all_gather.19 = bf16[2048,128]{1,0:T(8,128)(2,1)S(1)} all-gather(bf16[256,128]{1,0:T(8,128)(2,1)S(1)} %bitcast.45), channel_id=1, replica_groups=mesh['seq'=8,'head'=4] {'seq'}, dimensions={0}, use_global_device_ids=true | all-gather | bytes 589824 | tf_op jit(solution)/shard_map/all_gather | solution.py:179
  137.1 3.3 %while.56 = (s32[]{:T(128)}, f32[256,128]{1,0:T(8,128)S(1)}, f32[256]{0:T(256)S(1)}, f32[256]{0:T(256)S(1)}, s32[]{:T(128)}, /*index=5*/bf16[2048,128]{1,0:T(8,1...) while((s32[]{:T(128)}, f32[256,128]{1,0:T(8,128)S(1)}, ...), condition=%wide.region_5.6_spmd.clone, body=%wide.region_0.5_spmd.clone.sunk | while | flops 139006736 | bytes 4045177 | solution.py:62
  137.1 3.1 %conditional.10 = ((f32[256,128]{1,0:T(8,128)S(1)}, f32[256]{0:T(256)S(1)}, f32[256]{0:T(256)S(1)})) conditional(s32[]{:T(128)} %convert_element_type.68, (f32[256,128]{1,0:T(8,128)S(1)}, f32[256]{0:T(256)S(1)}, f32[256]{0:T(256)S(1)}) %tuple.145, (s32[]{:T(128)}, s32[]{:T(128)}, bf16[2048,128]{1,0:T(8,128)(2,1)S(1)}, bf16[256,128]{1,0:T(8,128)(2,1)}, ...), branch_computations={%region_1.0_spmd, %region_2.4_spmd} | conditional | flops 139006720 | bytes 4043862 | solution.py:50
  137.2 1.3 fusion.68
  138.5 0.8 fusion.8
  139.4 0.8 convolution_add_fusion
  140.3 0.7 multiply_reduce_fusion
  141.7 2.5 %while.57 = (s32[]{:T(128)}, f32[256,128]{1,0:T(8,128)S(1)}, s32[]{:T(128)}, bf16[2048,128]{1,0:T(8,128)(2,1)S(1)}, bf16[256,128]{1,0:T(8,128)(2,1)}, /*index=5*...) while((s32[]{:T(128)}, f32[256,128]{1,0:T(8,128)S(1)}, ...), condition=%wide.region_10.11_spmd.clone, body=%wide.region_7.10_spmd.clone.sunk | while | flops 203985168 | bytes 3296597 | solution.py:119
  141.7 2.4 %conditional.11 = (f32[256,128]{1,0:T(8,128)S(1)}) conditional(s32[]{:T(128)} %convert_element_type.69, f32[256,128]{1,0:T(8,128)S(1)} %get-tuple-element.1192, (s32[]{:T(128)}, s32[]{:T(128)}, bf16[2048,128]{1,0:T(8,128)(2,1)S(1)}, bf16[256,128]{1,0:T(8,128)(2,1)}, f32[256]{0:T(256)}, /*index=5*/bf16[2048,128]{1,0:T(8,128)(2,1)S(1)}, ...), branch_computations={%region_8.8_spmd, %region_9.9_spmd} | conditional | flops 203985152 | bytes 3295290 | solution.py:111
  142.3 1.3 fusion.30
  144.2 0.7 copy-done.6
  144.9 26.4 %all-gather = f32[8,1,256]{2,1,0:T(1,128)S(1)} all-gather(f32[1,1,256]{2,1,0:T(1,128)S(1)} %bitcast.52), channel_id=1, replica_groups=mesh['seq'=8,'head'=4] {'seq'}, dimensions={0}, use_global_device_ids=true | all-gather | bytes 9216 | tf_op jit(solution)/shard_map/all_gather | solution.py:199
  171.4 16.3 %all-gather.1 = f32[8,1,256]{2,1,0:T(1,128)S(1)} all-gather(f32[1,1,256]{2,1,0:T(1,128)S(1)} %bitcast.51), channel_id=1, replica_groups=mesh['seq'=8,'head'=4] {'seq'}, dimensions={0}, use_global_device_ids=true | all-gather | bytes 9216 | tf_op jit(solution)/shard_map/all_gather | solution.py:200
  187.7 3.1 %while.58 = (s32[]{:T(128)}, f32[256,128]{1,0:T(8,128)S(1)}, f32[256,128]{1,0:T(8,128)S(1)}, s32[]{:T(128)}, bf16[2048,128]{1,0:T(8,128)(2,1)S(1)}, /*index=5*/b...) while((s32[]{:T(128)}, f32[256,128]{1,0:T(8,128)S(1)}, ...), condition=%wide.region_14.15_spmd.clone.clone, body=%wide.region_11.14_spmd.clone.clone.sunk | while | flops 270861568 | bytes 4887901 | solution.py:167
  187.7 1.5 conditional.12
  188.2 0.7 fusion.53
  189.3 1.5 conditional.12
  189.8 0.7 fusion.53
  (53 shorter events, 5.3 us)
Async XLA Ops:
  0.6 0.8 copy-start
  2.1 69.0 %all-to-all-start = ((bf16[64,4,128]{2,0,1:T(8,128)(2,1)}), bf16[64,4,128]{2,0,1:T(8,128)(2,1)S(1)}, u32[]{:S(2)}, u32[]{:S(2)}) async-start(bf16[64,4,128]{2,0,1:T(8,128)(2,1)} %copy_bitcast_fusion.1), calls=%async_computation | async-start | bytes 131072 | tf_op jit(solution)/shard_map/all_to_all | solution.py:174
  6.4 32.7 %copy-start.4 = (bf16[256,128]{1,0:T(8,128)(2,1)S(1)}, bf16[256,128]{1,0:T(8,128)(2,1)}, u32[]{:S(2)}) copy-start(bf16[256,128]{1,0:T(8,128)(2,1)} %param.19) | copy-start | bytes 196612
  39.1 31.3 %copy-start.5 = (bf16[64,512]{1,0:T(8,128)(2,1)S(1)}, bf16[64,512]{1,0:T(8,128)(2,1)}, u32[]{:S(2)}) copy-start(bf16[64,512]{1,0:T(8,128)(2,1)} %param.18) | copy-start | bytes 196612
  71.1 34.5 %all-to-all-start.1 = ((bf16[64,4,128]{2,0,1:T(8,128)(2,1)}), bf16[64,4,128]{2,0,1:T(8,128)(2,1)S(1)}, u32[]{:S(2)}, u32[]{:S(2)}) async-start(bf16[64,4,128]{2,0,1:T(8,128)(2,1)} %copy_bitcast_fusion), calls=%async_computation.1 | async-start | bytes 131072 | tf_op jit(solution)/shard_map/all_to_all | solution.py:175
  144.2 43.5 %copy-start.3 = (f32[256,128]{1,0:T(8,128)}, f32[256,128]{1,0:T(8,128)S(1)}, u32[]{:S(2)}) copy-start(f32[256,128]{1,0:T(8,128)S(1)} %get-tuple-element.755) | copy-start | bytes 393220
  144.2 0.7 copy-start.6
  190.8 0.7 copy-start.1
  190.8 0.7 copy-start.2
where the time goes:
time: 192 us
  blocking collectives  169 us (88%)
  starting transfers between devices  7.55 us (4%)
  matrix products  6.85 us (4%)
  local copies, waits for them, and re-layouts  3.62 us (2%)
  other arithmetic  2.79 us (1%)
    all_gather x1, blocking collectives, per_device(): lax.all_gather(queries, 'seq', axis=0, tiled=True)  32.7 us
    all_gather x1, blocking collectives, per_device(): lax.all_gather(local_values, 'seq', axis=0, tiled=True)  31.5 us
    all_gather x1, blocking collectives, per_device(): lax.all_gather(out_grad, 'seq', axis=0, tiled=True)  31.3 us
    all_gather x1, blocking collectives, per_device(): lax.all_gather(local_keys, 'seq', axis=0, tiled=True)  31.2 us
    all_gather x1, blocking collectives, per_device(): lax.all_gather(log_norm, 'seq', axis=0, tiled=True)  26.4 us
    all_gather x1, blocking collectives, per_device(): lax.all_gather(row_delta, 'seq', axis=0, tiled=True)  16.3 us
    all_to_all x1, starting transfers between devices, per_device(): lax.all_to_all(keys, 'head', split_axis=1, concat_axis=0, tiled=True)  4.26 us
  transfers between devices with their start and end apart: 2, of which 0 were waited for; matrix products, arithmetic and copies ran while one was open for 0% of the time, Pallas kernels for 0%

commit v1 on v0

v1 whole, which is shorter than its diff:
```python
import functools
import math

import jax
import jax.numpy as jnp
from jax import lax
from jax.experimental import pallas as pl
from jax.experimental.pallas import tpu as pltpu
from jax.sharding import PartitionSpec as P

MESH = pl.DeviceIdType.MESH
masked_value = -1e30
NT = (((1,), (1,)), ((), ()))
NN = (((1,), (0,)), ((), ()))


def dot(a, b, dims):
    return lax.dot_general(a, b, dims, preferred_element_type=jnp.float32)


def row_width(shards):
    width = max(1, math.isqrt(shards // 2))
    while shards % width:
        width -= 1
    return width


def kernel(
    S, X, H, scaling,
    q_ref, k_ref, v_ref, g_ref,
    att_ref, dq_ref, dk_ref, dv_ref,
    kv, qd, stats, acc, top, total,
    local_sem, swap_send, swap_recv, up_send, side_send, block_recv, stat_send, stat_recv,
):
    Z = S // X
    rows, width = q_ref.shape
    part = k_ref.shape[0]
    me, head = lax.axis_index("seq"), lax.axis_index("head")
    z, x = lax.div(me, X), lax.rem(me, X)

    own_rows = pl.ds(pl.multiple_of(head * part, part), part)

    def columns(number):
        return pl.ds(pl.multiple_of(number * width, width), width)

    local = [
        pltpu.make_async_copy(q_ref, qd.at[me, 0], local_sem.at[0]),
        pltpu.make_async_copy(g_ref, qd.at[me, 1], local_sem.at[1]),
        pltpu.make_async_copy(k_ref.at[:, columns(head)], kv.at[me, 0, own_rows], local_sem.at[2]),
        pltpu.make_async_copy(v_ref.at[:, columns(head)], kv.at[me, 1, own_rows], local_sem.at[3]),
    ]
    for copy in local:
        copy.start()

    barrier = pltpu.get_barrier_semaphore()
    for step in range(1, S):
        pl.semaphore_signal(
            barrier, inc=1, device_id={"seq": lax.rem(me + step, S)}, device_id_type=MESH
        )
    for step in range(1, H):
        pl.semaphore_signal(
            barrier, inc=1, device_id={"head": lax.rem(head + step, H)}, device_id_type=MESH
        )
    pl.semaphore_wait(barrier, S + H - 2)

    swaps = []
    for step in range(1, H):
        other = lax.rem(head + step, H)
        for kind, ref in enumerate((k_ref, v_ref)):
            swaps.append(
                pltpu.make_async_remote_copy(
                    src_ref=ref.at[:, columns(other)],
                    dst_ref=kv.at[me, kind, own_rows],
                    send_sem=swap_send.at[kind, step],
                    recv_sem=swap_recv.at[kind, step],
                    device_id={"head": other},
                    device_id_type=MESH,
                )
            )
    for copy in swaps:
        copy.start()

    buffers = (kv, qd)

    def along(kind, t):
        zb = z - t if kind == 0 else z + t
        b = zb * X + x
        target = me + X if kind == 0 else me - X
        needed = (z < Z - 1) if kind == 0 else (z > 0)
        copy = pltpu.make_async_remote_copy(
            src_ref=buffers[kind].at[b],
            dst_ref=buffers[kind].at[b],
            send_sem=up_send.at[kind, t],
            recv_sem=block_recv.at[kind, b],
            device_id={"seq": target},
            device_id_type=MESH,
        )
        return needed, copy

    def beside(kind, t, step):
        zb = z - t if kind == 0 else z + t
        b = zb * X + x
        other = lax.rem(x + step, X)
        needed = (t > 0) | ((other > x) if kind == 0 else (other < x))
        copy = pltpu.make_async_remote_copy(
            src_ref=buffers[kind].at[b],
            dst_ref=buffers[kind].at[b],
            send_sem=side_send.at[kind, t, step],
            recv_sem=block_recv.at[kind, b],
            device_id={"seq": z * X + other},
            device_id_type=MESH,
        )
        return needed, copy

    def outgoing(kind, t):
        return [along(kind, t)] + [beside(kind, t, step) for step in range(1, X)]

    def send_on(kind, t):
        for needed, copy in outgoing(kind, t):
            @pl.when(needed)
            def _(copy=copy):
                copy.start()

    def arrived(kind, b):
        pltpu.make_async_copy(
            buffers[kind].at[b], buffers[kind].at[b], block_recv.at[kind, b]
        ).wait()

    local[0].wait()
    local[1].wait()
    send_on(1, 0)
    for copy in local[2:]:
        copy.wait()
    for copy in swaps:
        copy.wait_recv()
    send_on(0, 0)

    def forward(b, diagonal):
        s = dot(qd[me, 0], kv[b, 0], NT) * scaling
        if diagonal:
            r = lax.broadcasted_iota(jnp.int32, (rows, rows), 0)
            c = lax.broadcasted_iota(jnp.int32, (rows, rows), 1)
            s = jnp.where(c <= r, s, masked_value)
            high = jnp.max(s, axis=1, keepdims=True)
        else:
            old = top[:, :1]
            high = jnp.maximum(old, jnp.max(s, axis=1, keepdims=True))
        p = jnp.exp(s - high)
        psum = jnp.sum(p, axis=1, keepdims=True)
        pv = dot(p.astype(jnp.bfloat16), kv[b, 1], NN)
        if diagonal:
            total[...] = jnp.broadcast_to(psum, total.shape)
            acc[...] = pv
        else:
            factor = jnp.exp(old - high)
            total[...] = total[...] * factor + psum
            acc[...] = acc[...] * factor + pv
        top[...] = jnp.broadcast_to(high, top.shape)

    forward(me, True)

    def relay(t, carry):
        up = z - t >= 0
        down = z + t < Z

        @pl.when(up)
        def _():
            arrived(0, (z - t) * X + x)
            send_on(0, t)

        @pl.when(down)
        def _():
            arrived(1, (z + t) * X + x)
            send_on(1, t)

        @pl.when(up)
        def _():
            forward((z - t) * X + x, False)

        for step in range(1, X):
            other = lax.rem(x + step, X)

            @pl.when((z - (t - 1) >= 0) & ((t > 1) | (other < x)))
            def _(other=other):
                b = (z - (t - 1)) * X + other
                arrived(0, b)
                forward(b, False)

        return carry

    lax.fori_loop(1, Z + 1, relay, 0)

    sums = total[:, :1]
    output = acc[...] / sums
    att_ref[...] = output.astype(att_ref.dtype)
    log_norm = top[:, :1] + jnp.log(sums)
    delta = jnp.sum(qd[me, 1].astype(jnp.float32) * output, axis=1, keepdims=True)
    top[...] = jnp.broadcast_to(log_norm, top.shape)
    total[...] = jnp.broadcast_to(delta, total.shape)
    stats[me, 0:4, :] = top[...].T[0:4]
    stats[me, 4:8, :] = total[...].T[0:4]

    def stat_copy(b):
        return pltpu.make_async_remote_copy(
            src_ref=stats.at[me],
            dst_ref=stats.at[me],
            send_sem=stat_send.at[b],
            recv_sem=stat_recv.at[me],
            device_id={"seq": b},
            device_id_type=MESH,
        )

    def stat_out(b, carry):
        stat_copy(b).start()
        return carry

    lax.fori_loop(0, me, stat_out, 0)

    def query_side(b, diagonal):
        s = dot(qd[me, 0], kv[b, 0], NT) * scaling
        p = jnp.exp(s - top[:, :1])
        if diagonal:
            r = lax.broadcasted_iota(jnp.int32, (rows, rows), 0)
            c = lax.broadcasted_iota(jnp.int32, (rows, rows), 1)
            p = jnp.where(c <= r, p, 0.0)
        gp = dot(qd[me, 1], kv[b, 1], NT)
        gs = (p * (gp - total[:, :1]) * scaling).astype(jnp.bfloat16)
        return dot(gs, kv[b, 0], NN)

    dq_ref[...] = query_side(me, True)

    def query_step(b, carry):
        dq_ref[...] += query_side(b, False)
        return carry

    lax.fori_loop(0, me, query_step, 0)

    def key_side(b, diagonal):
        s = dot(kv[me, 0], qd[b, 0], NT) * scaling
        p = jnp.exp(s - stats[b, 0:1, :])
        if diagonal:
            r = lax.broadcasted_iota(jnp.int32, (rows, rows), 0)
            c = lax.broadcasted_iota(jnp.int32, (rows, rows), 1)
            p = jnp.where(r <= c, p, 0.0)
        gp = dot(kv[me, 1], qd[b, 1], NT)
        gs = (p * (gp - stats[b, 4:5, :]) * scaling).astype(jnp.bfloat16)
        return dot(gs, qd[b, 0], NN), dot(p.astype(jnp.bfloat16), qd[b, 1], NN)

    dk, dv = key_side(me, True)
    dk_ref[...] = dk
    dv_ref[...] = dv

    def key_step(b, carry):
        @pl.when(lax.rem(b, X) != x)
        def _():
            arrived(1, b)

        pltpu.make_async_copy(stats.at[b], stats.at[b], stat_recv.at[b]).wait()
        dk, dv = key_side(b, False)
        dk_ref[...] += dk
        dv_ref[...] += dv
        return carry

    lax.fori_loop(me + 1, S, key_step, 0)

    for copy in swaps:
        copy.wait_send()

    def drain(t, carry):
        for kind in range(2):
            present = (z - t >= 0) if kind == 0 else (z + t < Z)
            for needed, copy in outgoing(kind, t):
                @pl.when(present & needed)
                def _(copy=copy):
                    copy.wait_send()
        return carry

    lax.fori_loop(0, Z, drain, 0)

    def stat_drain(b, carry):
        stat_copy(b).wait_send()
        return carry

    lax.fori_loop(0, me, stat_drain, 0)


def solution(mesh):
    S, H = mesh.shape["seq"], mesh.shape["head"]
    X = row_width(S)
    Z = S // X

    def step(queries, keys, values, out_grad):
        rows, width = queries.shape
        f32 = jax.ShapeDtypeStruct((rows, width), jnp.float32)
        DMA = pltpu.SemaphoreType.DMA
        return pl.pallas_call(
            functools.partial(kernel, S, X, H, 1.0 / math.sqrt(width)),
            out_shape=(jax.ShapeDtypeStruct((rows, width), jnp.bfloat16), f32, f32, f32),
            in_specs=[pl.BlockSpec(memory_space=pl.ANY)] * 4,
            out_specs=(pl.BlockSpec(memory_space=pltpu.VMEM),) * 4,
            scratch_shapes=[
                pltpu.VMEM((S, 2, rows, width), jnp.bfloat16),
                pltpu.VMEM((S, 2, rows, width), jnp.bfloat16),
                pltpu.VMEM((S, 8, rows), jnp.float32),
                pltpu.VMEM((rows, width), jnp.float32),
                pltpu.VMEM((rows, 128), jnp.float32),
                pltpu.VMEM((rows, 128), jnp.float32),
                DMA((4,)),
                DMA((2, H)),
                DMA((2, H)),
                DMA((2, Z)),
                DMA((2, Z, X)),
                DMA((2, S)),
                DMA((S,)),
                DMA((S,)),
            ],
            compiler_params=pltpu.CompilerParams(collective_id=0, has_side_effects=True),
            name="ring_attention",
        )(queries, keys, values, out_grad)

    return jax.shard_map(
        step,
        mesh=mesh,
        in_specs=(
            P("seq", "head"),
            P(("seq", "head"), None),
            P(("seq", "head"), None),
            P("seq", "head"),
        ),
        out_specs=(P("seq", "head"),) * 4,
        check_vma=False,
    )
```

time: 192 us -> 38.7 us (0.20)
  blocking collectives: 169 us -> 0 us
  Pallas kernels: 0 us -> 33.8 us
  starting transfers between devices: 7.55 us -> 0 us
  matrix products: 6.85 us -> 0 us
  other arithmetic: 2.79 us -> 0 us
    all_gather x6 -> x0, blocking collectives: 169 us -> none  [the longest x1 32.7 us: per_device(): lax.all_gather(queries, 'seq', axis=0, tiled=True)]
    pallas_call x0 -> x1, Pallas kernels: none -> 33.8 us  [step(): pl.pallas_call(functools.partial(kernel, S, X, H, 1.0 / math.sqrt(width))...]
    all_to_all x2 -> x0, starting transfers between devices: 7.55 us -> none  [the longest x1 4.26 us: per_device(): lax.all_to_all(keys, 'head', split_axis=1, concat_axis=0, tiled=True)]
    dot_general x10 -> x0, matrix products: 6.85 us -> none  [the longest x2 1.35 us: key_compute(): jnp.einsum('qk,qd->kd', grad_scores, query_piece, preferred_element_type=...]
    unnamed x14 -> x10, local copies, waits for them, and re-layouts: 2.23 us -> 4.07 us
  transfers between devices with their start and end apart: 2 -> 0, of which waited for: 0 -> 0; matrix products, arithmetic and copies ran while one was open for 0% -> 0% of each run, Pallas kernels for 0% -> 0%
where the time goes in v1:
time: 38.7 us; the launch traced here: 38.5 us
  Pallas kernels  33.8 us (87%)
  local copies, waits for them, and re-layouts  4.07 us (11%)
  between operations  0.65 us (2%)
    pallas_call x1, Pallas kernels, step(): pl.pallas_call(functools.partial(kernel, S, X, H, 1.0 / math.sqrt(width))...  33.8 us
    unnamed x10, local copies, waits for them, and re-layouts  4.07 us

profile of v1, /device:TPU:0, one launch (start us, length us, event | category | flops | bytes accessed | tf_op | source)
XLA Modules:
  0.0 38.5 jit_solution(14483880166564493081)
XLA Ops:
  0.6 33.8 %ring_attention.1 = (bf16[256,128]{1,0:T(8,128)(2,1)}, f32[256,128]{1,0:T(8,128)}, f32[256,128]{1,0:T(8,128)}, f32[256,128]{1,0:T(8,128)}) custom-call(bf16[256,128]{1,0:T(8,128)(2,1)} %q_ref.1, bf16[64,512]{1,0:T(8,128)(2,1)} %k_ref.1, bf16[64,512]{1,0:T(8,128)(2,1)} %v_ref.1, bf16[256,128]{1,0:T(8,128)(2,1)} %g_ref.1), custom_call_target="tpu_custom_call" | custom-call | tf_op jit(solution)/shard_map/ring_attention/pallas_call | solution.py:296
  34.4 0.0 copy-start.2
  34.4 1.5 %copy.12 = bf16[256,128]{1,0:T(8,128)(2,1)} copy(bf16[256,128]{1,0:T(8,128)(2,1)} %get-tuple-element.8) | data formatting | bytes 131072
  35.9 0.0 copy-done.2
  35.9 0.0 copy-start.1
  35.9 0.7 %copy.13 = f32[256,128]{1,0:T(8,128)} copy(f32[256,128]{1,0:T(8,128)S(1)} %copy-done.2) | data formatting | bytes 262144
  36.6 0.3 copy-done.1
  36.9 0.0 copy-start
  36.9 0.7 %copy.14 = f32[256,128]{1,0:T(8,128)} copy(f32[256,128]{1,0:T(8,128)S(1)} %copy-done.1) | data formatting | bytes 262144
  37.5 0.3 copy-done
  37.8 0.7 %copy.15 = f32[256,128]{1,0:T(8,128)} copy(f32[256,128]{1,0:T(8,128)S(1)} %copy-done) | data formatting | bytes 262144
Async XLA Ops:
  34.4 1.5 %copy-start.2 = (f32[256,128]{1,0:T(8,128)S(1)}, f32[256,128]{1,0:T(8,128)}, u32[]{:S(2)}) copy-start(f32[256,128]{1,0:T(8,128)} %get-tuple-element.9) | copy-start | bytes 393220
  35.9 1.0 %copy-start.1 = (f32[256,128]{1,0:T(8,128)S(1)}, f32[256,128]{1,0:T(8,128)}, u32[]{:S(2)}) copy-start(f32[256,128]{1,0:T(8,128)} %get-tuple-element.10) | copy-start | bytes 393220
  36.9 1.0 %copy-start = (f32[256,128]{1,0:T(8,128)S(1)}, f32[256,128]{1,0:T(8,128)}, u32[]{:S(2)}) copy-start(f32[256,128]{1,0:T(8,128)} %get-tuple-element.11) | copy-start | bytes 393220

commit v2 on v1

--- a/solution.py
+++ b/solution.py
@@ -23,6 +23,16 @@
     while shards % width:
         width -= 1
     return width
+
+
+def partner(head, step, count):
+    if count & (count - 1):
+        return lax.rem(step + count - head, count)
+    other, bit = 0, 1
+    while bit < count:
+        other = other + bit * lax.rem(lax.div(head, bit) + step // bit, 2)
+        bit *= 2
+    return other
 
 
 def kernel(
@@ -53,19 +63,25 @@
         copy.start()
 
     barrier = pltpu.get_barrier_semaphore()
-    for step in range(1, S):
+    above, below = z < Z - 1, z > 0
+    for there, target in ((above, me + X), (below, me - X)):
+        @pl.when(there)
+        def _(target=target):
+            pl.semaphore_signal(barrier, inc=1, device_id={"seq": target}, device_id_type=MESH)
+    for step in range(1, X):
         pl.semaphore_signal(
-            barrier, inc=1, device_id={"seq": lax.rem(me + step, S)}, device_id_type=MESH
+            barrier, inc=1, device_id={"seq": z * X + lax.rem(x + step, X)}, device_id_type=MESH
         )
     for step in range(1, H):
         pl.semaphore_signal(
-            barrier, inc=1, device_id={"head": lax.rem(head + step, H)}, device_id_type=MESH
+            barrier, inc=1, device_id={"head": partner(head, step, H)}, device_id_type=MESH
         )
-    pl.semaphore_wait(barrier, S + H - 2)
+    peers = X + H - 2 + lax.convert_element_type(above, jnp.int32)
+    pl.semaphore_wait(barrier, peers + lax.convert_element_type(below, jnp.int32))
 
     swaps = []
     for step in range(1, H):
-        other = lax.rem(head + step, H)
+        other = partner(head, step, H)
         for kind, ref in enumerate((k_ref, v_ref)):
             swaps.append(
                 pltpu.make_async_remote_copy(
@@ -82,58 +98,62 @@
 
     buffers = (kv, qd)
 
-    def along(kind, t):
+    def piece(kind, b, step):
+        start = pl.multiple_of(partner(head, step, H) * part, part)
+        return buffers[kind].at[b, :, pl.ds(start, part)]
+
+    def outgoing(kind, t, c):
         zb = z - t if kind == 0 else z + t
         b = zb * X + x
-        target = me + X if kind == 0 else me - X
-        needed = (z < Z - 1) if kind == 0 else (z > 0)
-        copy = pltpu.make_async_remote_copy(
-            src_ref=buffers[kind].at[b],
-            dst_ref=buffers[kind].at[b],
-            send_sem=up_send.at[kind, t],
-            recv_sem=block_recv.at[kind, b],
-            device_id={"seq": target},
-            device_id_type=MESH,
-        )
-        return needed, copy
-
-    def beside(kind, t, step):
-        zb = z - t if kind == 0 else z + t
-        b = zb * X + x
-        other = lax.rem(x + step, X)
-        needed = (t > 0) | ((other > x) if kind == 0 else (other < x))
-        copy = pltpu.make_async_remote_copy(
-            src_ref=buffers[kind].at[b],
-            dst_ref=buffers[kind].at[b],
-            send_sem=side_send.at[kind, t, step],
-            recv_sem=block_recv.at[kind, b],
-            device_id={"seq": z * X + other},
-            device_id_type=MESH,
-        )
-        return needed, copy
-
-    def outgoing(kind, t):
-        return [along(kind, t)] + [beside(kind, t, step) for step in range(1, X)]
-
-    def send_on(kind, t):
-        for needed, copy in outgoing(kind, t):
+        chunk = piece(kind, b, c)
+
+        def copy_to(target, send_sem):
+            return pltpu.make_async_remote_copy(
+                src_ref=chunk,
+                dst_ref=chunk,
+                send_sem=send_sem,
+                recv_sem=block_recv.at[kind, b, c],
+                device_id={"seq": target},
+                device_id_type=MESH,
+            )
+
+        copies = [
+            (
+                above if kind == 0 else below,
+                copy_to(me + X if kind == 0 else me - X, up_send.at[kind, t, c]),
+            )
+        ]
+        for step in range(1, X):
+            other = lax.rem(x + step, X)
+            needed = (t > 0) | ((other > x) if kind == 0 else (other < x))
+            copies.append((needed, copy_to(z * X + other, side_send.at[kind, t, step, c])))
+        return copies
+
+    def send_on(kind, t, c):
+        for needed, copy in outgoing(kind, t, c):
             @pl.when(needed)
             def _(copy=copy):
                 copy.start()
 
-    def arrived(kind, b):
-        pltpu.make_async_copy(
-            buffers[kind].at[b], buffers[kind].at[b], block_recv.at[kind, b]
-        ).wait()
-
+    def arrived(kind, b, c):
+        chunk = piece(kind, b, c)
+        pltpu.make_async_copy(chunk, chunk, block_recv.at[kind, b, c]).wait()
+
+    def all_arrived(kind, b):
+        for c in range(H):
+            arrived(kind, b, c)
+
+    local[2].wait()
+    local[3].wait()
+    send_on(0, 0, 0)
     local[0].wait()
     local[1].wait()
-    send_on(1, 0)
-    for copy in local[2:]:
-        copy.wait()
-    for copy in swaps:
-        copy.wait_recv()
-    send_on(0, 0)
+    for c in range(H):
+        send_on(1, 0, c)
+    for c in range(1, H):
+        swaps[2 * c - 2].wait_recv()
+        swaps[2 * c - 1].wait_recv()
+        send_on(0, 0, c)
 
     def forward(b, diagonal):
         s = dot(qd[me, 0], kv[b, 0], NT) * scaling
@@ -163,15 +183,16 @@
         up = z - t >= 0
         down = z + t < Z
 
-        @pl.when(up)
-        def _():
-            arrived(0, (z - t) * X + x)
-            send_on(0, t)
-
-        @pl.when(down)
-        def _():
-            arrived(1, (z + t) * X + x)
-            send_on(1, t)
+        for c in range(H):
+            @pl.when(up)
+            def _():
+                arrived(0, (z - t) * X + x, c)
+                send_on(0, t, c)
+
+            @pl.when(down)
+            def _():
+                arrived(1, (z + t) * X + x, c)
+                send_on(1, t, c)
 
         @pl.when(up)
         def _():
@@ -183,7 +204,7 @@
             @pl.when((z - (t - 1) >= 0) & ((t > 1) | (other < x)))
             def _(other=other):
                 b = (z - (t - 1)) * X + other
-                arrived(0, b)
+                all_arrived(0, b)
                 forward(b, False)
 
         return carry
@@ -253,7 +274,7 @@
     def key_step(b, carry):
         @pl.when(lax.rem(b, X) != x)
         def _():
-            arrived(1, b)
+            all_arrived(1, b)
 
         pltpu.make_async_copy(stats.at[b], stats.at[b], stat_recv.at[b]).wait()
         dk, dv = key_side(b, False)
@@ -269,10 +290,11 @@
     def drain(t, carry):
         for kind in range(2):
             present = (z - t >= 0) if kind == 0 else (z + t < Z)
-            for needed, copy in outgoing(kind, t):
-                @pl.when(present & needed)
-                def _(copy=copy):
-                    copy.wait_send()
+            for c in range(H):
+                for needed, copy in outgoing(kind, t, c):
+                    @pl.when(present & needed)
+                    def _(copy=copy):
+                        copy.wait_send()
         return carry
 
     lax.fori_loop(0, Z, drain, 0)
@@ -308,9 +330,9 @@
                 DMA((4,)),
                 DMA((2, H)),
                 DMA((2, H)),
-                DMA((2, Z)),
-                DMA((2, Z, X)),
-                DMA((2, S)),
+                DMA((2, Z, H)),
+                DMA((2, Z, X, H)),
+                DMA((2, S, H)),
                 DMA((S,)),
                 DMA((S,)),
             ],

time: 38.7 us -> 33.3 us (0.86)
  Pallas kernels: 33.8 us -> 28.4 us
    pallas_call x1, Pallas kernels: 33.8 us -> 28.4 us  [step(): pl.pallas_call(functools.partial(kernel, S, X, H, 1.0 / math.sqrt(width))...]
where the time goes in v2:
time: 33.3 us; the launch traced here: 33.1 us
  Pallas kernels  28.4 us (85%)
  local copies, waits for them, and re-layouts  4.07 us (12%)
  between operations  0.65 us (2%)
    pallas_call x1, Pallas kernels, step(): pl.pallas_call(functools.partial(kernel, S, X, H, 1.0 / math.sqrt(width))...  28.4 us
    unnamed x10, local copies, waits for them, and re-layouts  4.07 us

profile of v2, /device:TPU:0, one launch (start us, length us, event | category | flops | bytes accessed | tf_op | source)
XLA Modules:
  0.0 33.1 jit_solution(6054353110893771806)
XLA Ops:
  0.6 28.4 %ring_attention.1 = (bf16[256,128]{1,0:T(8,128)(2,1)}, f32[256,128]{1,0:T(8,128)}, f32[256,128]{1,0:T(8,128)}, f32[256,128]{1,0:T(8,128)}) custom-call(bf16[256,128]{1,0:T(8,128)(2,1)} %q_ref.1, bf16[64,512]{1,0:T(8,128)(2,1)} %k_ref.1, bf16[64,512]{1,0:T(8,128)(2,1)} %v_ref.1, bf16[256,128]{1,0:T(8,128)(2,1)} %g_ref.1), custom_call_target="tpu_custom_call" | custom-call | tf_op jit(solution)/shard_map/ring_attention/pallas_call | solution.py:318
  29.0 0.0 copy-start.2
  29.0 1.5 %copy.12 = bf16[256,128]{1,0:T(8,128)(2,1)} copy(bf16[256,128]{1,0:T(8,128)(2,1)} %get-tuple-element.8) | data formatting | bytes 131072
  30.5 0.0 copy-done.2
  30.5 0.0 copy-start.1
  30.5 0.7 %copy.13 = f32[256,128]{1,0:T(8,128)} copy(f32[256,128]{1,0:T(8,128)S(1)} %copy-done.2) | data formatting | bytes 262144
  31.2 0.3 copy-done.1
  31.5 0.0 copy-start
  31.5 0.7 %copy.14 = f32[256,128]{1,0:T(8,128)} copy(f32[256,128]{1,0:T(8,128)S(1)} %copy-done.1) | data formatting | bytes 262144
  32.1 0.3 copy-done
  32.4 0.7 %copy.15 = f32[256,128]{1,0:T(8,128)} copy(f32[256,128]{1,0:T(8,128)S(1)} %copy-done) | data formatting | bytes 262144
Async XLA Ops:
  29.0 1.5 %copy-start.2 = (f32[256,128]{1,0:T(8,128)S(1)}, f32[256,128]{1,0:T(8,128)}, u32[]{:S(2)}) copy-start(f32[256,128]{1,0:T(8,128)} %get-tuple-element.9) | copy-start | bytes 393220
  30.5 1.0 %copy-start.1 = (f32[256,128]{1,0:T(8,128)S(1)}, f32[256,128]{1,0:T(8,128)}, u32[]{:S(2)}) copy-start(f32[256,128]{1,0:T(8,128)} %get-tuple-element.10) | copy-start | bytes 393220
  31.5 1.0 %copy-start = (f32[256,128]{1,0:T(8,128)S(1)}, f32[256,128]{1,0:T(8,128)}, u32[]{:S(2)}) copy-start(f32[256,128]{1,0:T(8,128)} %get-tuple-element.11) | copy-start | bytes 393220

commit v3 on v2

--- a/solution.py
+++ b/solution.py
@@ -306,6 +306,12 @@
     lax.fori_loop(0, me, stat_drain, 0)
 
 
+def finish(*refs):
+    half = len(refs) // 2
+    for source, target in zip(refs[:half], refs[half:]):
+        target[...] = source[...]
+
+
 def solution(mesh):
     S, H = mesh.shape["seq"], mesh.shape["head"]
     X = row_width(S)
@@ -315,10 +321,12 @@
         rows, width = queries.shape
         f32 = jax.ShapeDtypeStruct((rows, width), jnp.float32)
         DMA = pltpu.SemaphoreType.DMA
-        return pl.pallas_call(
+        grant = 8 * 2**20 + 16 * S * rows * width
+        shapes = (jax.ShapeDtypeStruct((rows, width), jnp.bfloat16), f32, f32, f32)
+        results = pl.pallas_call(
             functools.partial(kernel, S, X, H, 1.0 / math.sqrt(width)),
             out_shape=(jax.ShapeDtypeStruct((rows, width), jnp.bfloat16), f32, f32, f32),
-            in_specs=[pl.BlockSpec(memory_space=pl.ANY)] * 4,
+            in_specs=[pl.BlockSpec(memory_space=pltpu.HBM)] * 4,
             out_specs=(pl.BlockSpec(memory_space=pltpu.VMEM),) * 4,
             scratch_shapes=[
                 pltpu.VMEM((S, 2, rows, width), jnp.bfloat16),
@@ -336,9 +344,17 @@
                 DMA((S,)),
                 DMA((S,)),
             ],
-            compiler_params=pltpu.CompilerParams(collective_id=0, has_side_effects=True),
+            compiler_params=pltpu.CompilerParams(collective_id=0, has_side_effects=True, vmem_limit_bytes=grant),
             name="ring_attention",
-        )(queries, keys, values, out_grad)
+        )(*(pltpu.with_memory_space_constraint(a, pltpu.HBM) for a in (queries, keys, values, out_grad)))
+        return pl.pallas_call(
+            finish,
+            out_shape=shapes,
+            in_specs=[pl.BlockSpec(memory_space=pltpu.VMEM)] * 4,
+            out_specs=(pl.BlockSpec(memory_space=pltpu.VMEM),) * 4,
+            compiler_params=pltpu.CompilerParams(vmem_limit_bytes=grant),
+            name="finish",
+        )(*results)
 
     return jax.shard_map(
         step,

time: 33.3 us -> 29.2 us (0.88)
  local copies, waits for them, and re-layouts: 4.07 us -> 0 us
    unnamed x10 -> x0, local copies, waits for them, and re-layouts: 4.07 us -> none
    pallas_call x0 -> x1, Pallas kernels: none -> 0.8 us  [step(): pl.pallas_call(finish, out_shape=shapes, in_specs=[pl.BlockSpec(memory_sp...]
    pallas_call x1, Pallas kernels: 28.4 us -> 27.6 us  [step(): pl.pallas_call(functools.partial(kernel, S, X, H, 1.0 / math.sqrt(width))...]
where the time goes in v3:
time: 29.2 us; the launch traced here: 29 us
  Pallas kernels  28.4 us (97%)
  between operations  0.64 us (2%)
    pallas_call x1, Pallas kernels, step(): pl.pallas_call(functools.partial(kernel, S, X, H, 1.0 / math.sqrt(width))...  27.6 us
    pallas_call x1, Pallas kernels, step(): pl.pallas_call(finish, out_shape=shapes, in_specs=[pl.BlockSpec(memory_sp...  0.8 us

profile of v3, /device:TPU:0, one launch (start us, length us, event | category | flops | bytes accessed | tf_op | source)
XLA Modules:
  0.0 29.0 jit_solution(8320170925906277056)
XLA Ops:
  0.6 27.6 %ring_attention.1 = (bf16[256,128]{1,0:T(8,128)(2,1)S(1)}, f32[256,128]{1,0:T(8,128)S(1)}, f32[256,128]{1,0:T(8,128)S(1)}, f32[256,128]{1,0:T(8,128)S(1)}) custom-call(bf16[256,128]{1,0:T(8,128)(2,1)} %q_ref.1, bf16[64,512]{1,0:T(8,128)(2,1)} %k_ref.1, bf16[64,512]{1,0:T(8,128)(2,1)} %v_ref.1, bf16[256,128]{1,0:T(8,128)(2,1)} %g_ref.1), custom_call_target="tpu_custom_call" | custom-call | tf_op jit(solution)/shard_map/ring_attention/pallas_call | solution.py:326
  28.2 0.8 %finish.1 = (bf16[256,128]{1,0:T(8,128)(2,1)}, f32[256,128]{1,0:T(8,128)}, f32[256,128]{1,0:T(8,128)}, f32[256,128]{1,0:T(8,128)}) custom-call(bf16[256,128]{1,0:T(8,128)(2,1)S(1)} %get-tuple-element.8.refs_0_, f32[256,128]{1,0:T(8,128)S(1)} %get-tuple-element.9.refs_1_, f32[256,128]{1,0:T(8,128)S(1)} %get-tuple-element.10.refs_2_, ...), custom_call_target="tpu_custom_call" | custom-call | tf_op jit(solution)/shard_map/finish/pallas_call | solution.py:350
